TPU v7x, 32 devices: a whole 2x2x4 slice. The times are simulated.
32 devices in a mesh: pair: 16 (over z, x, core), virt: 2 (over y).
Axes of the slice: x: 2, y: 2, z: 4, core: 2. Of those that a mesh axis runs over, the one named last changes fastest.
Arguments:
- amplitudes: bfloat16 [96, 96, 128, 128], P('pair', None, 'virt'), may hold values from -6 to 6
- integrals: bfloat16 [128, 20, 128, 128], P('virt'), may hold values from -0.125 to 0.125
- cd_tiles: int32 [128, 20], P('virt'), may hold values from 0 to 127, as said below
- tile_counts: int32 [128], P('virt'), may hold values from 10 to 20, as said below
- eps_occ: float32 [96], replicated, may hold values from -2 to -0.5
- eps_virt: float32 [128], replicated, may hold values from 0.5 to 3
Outputs:
- new_amplitudes: bfloat16 [96, 96, 128, 128], P('pair', None, 'virt')
Inputs may be any that keep to these rules, and one draw needn't show every extreme that they name: `cd_tiles`: row a holds 20 different numbers from lo(a) to lo(a) + 2 * 64 - 1, where lo(a) = min(max(a - 64, 0), 0); only its first tile_counts[a] entries are live. `tile_counts`: some entry equals 20.
All inputs are finite; a program needn't handle non-finite values.
Results may differ from a plain program's by a relative error of at most 0.001.
Values may be sent and summed in bfloat16 or wider, within the bound.
A program may use at most 448 MiB of HBM per device.

v0:
```python
import jax
import jax.numpy as jnp
from jax import lax
from jax.sharding import PartitionSpec as P


def extended(cells, sides, width):
    for axis, dim in sides:
        count = lax.axis_size(axis)
        ends = count - 1
        head = lax.slice_in_dim(cells, 0, width, axis=dim)
        tail = lax.slice_in_dim(cells, cells.shape[dim] - width, cells.shape[dim], axis=dim)
        cells = jnp.concatenate(
            [
                lax.ppermute(tail, axis, [(i, (i + 1) % count) for i in range(ends)]),
                cells,
                lax.ppermute(head, axis, [((i + 1) % count, i) for i in range(ends)]),
            ],
            axis=dim,
        )
    return cells


def per_device(amplitudes, integrals, cd_tiles, tile_counts, eps_occ, eps_virt):
    own_rows = amplitudes.shape[0]
    own_tiles = amplitudes.shape[2]
    slot_count = integrals.shape[1]
    first_tile = lax.axis_index("virt") * own_tiles
    first_row = lax.axis_index("pair") * own_rows
    local_tiles = cd_tiles - first_tile + own_tiles
    slot_ids = lax.broadcasted_iota(jnp.int32, cd_tiles.shape, 1)
    kept_slots = (slot_ids < tile_counts[:, None]).astype(jnp.bfloat16)
    masked_weights = integrals * kept_slots[:, :, None, None]
    padded = extended(amplitudes, (("virt", 2),), own_tiles)
    block_width = min(4, slot_count)
    ladder = None
    for block_start in range(0, slot_count, block_width):
        block_stop = min(block_start + block_width, slot_count)
        columns = local_tiles[:, block_start:block_stop]
        picked = jnp.take(padded, columns, axis=2)
        weights = masked_weights[:, block_start:block_stop]
        term = jnp.einsum("ijasd,asdb->ijab", picked, weights, preferred_element_type=jnp.float32)
        ladder = term if ladder is None else ladder + term
    arrived_ladder = lax.all_to_all(
        lax.all_to_all(ladder, "pair", split_axis=1, concat_axis=0, tiled=True),
        "virt",
        split_axis=3,
        concat_axis=2,
        tiled=True,
    )
    partner = jnp.transpose(arrived_ladder, (1, 0, 3, 2))
    occupied_own = lax.dynamic_slice_in_dim(eps_occ, first_row, own_rows)
    virtual_own = lax.dynamic_slice_in_dim(eps_virt, first_tile, own_tiles)
    denominator = (
        occupied_own[:, None, None, None]
        + eps_occ[None, :, None, None]
        - virtual_own[None, None, :, None]
        - eps_virt[None, None, None, :]
    )
    return ((ladder + partner) / denominator).astype(jnp.bfloat16)


def solution(mesh):
    in_specs = (
        P("pair", None, "virt", None),
        P("virt", None, None, None),
        P("virt", None),
        P("virt"),
        P(),
        P(),
    )
    out_specs = P("pair", None, "virt", None)
    return jax.shard_map(
        per_device, mesh=mesh, in_specs=in_specs, out_specs=out_specs, check_vma=False
    )
```

profile of v0, /device:TPU:0, one launch (start us, length us, event | category | flops | bytes accessed | tf_op | source)
XLA Modules:
  0.0 1329.9 jit_solution(11712600738236134319)
XLA Ops:
  0.0 13.5 %copy.69 = bf16[6,96,64,128]{3,1,2,0:T(8,128)(2,1)} copy(bf16[6,96,64,128]{3,2,1,0:T(8,128)(2,1)} %param.8) | data formatting | bytes 18874368 | tf_op args[0]
  13.5 8.6 collective-permute-start
  22.0 1.5 collective-permute-start.1
  23.5 0.7 subtract_add_fusion
  24.2 0.1 copy.75
  24.3 0.1 reshape.119
  24.4 0.1 copy.78
  24.5 0.1 reshape.123
  24.7 0.1 copy.77
  24.8 0.7 copy.74
  25.5 0.1 copy.81
  25.6 0.1 reshape.127
  25.7 0.1 copy.84
  25.8 0.1 reshape.131
  25.9 0.7 copy.80
  26.6 0.1 copy.72
  26.7 0.1 reshape.115
  26.8 0.7 copy.68
  27.5 0.7 copy.83
  28.2 0.7 fusion.25
  29.0 28.2 %broadcast_multiply_fusion = bf16[64,20,128,128]{3,2,1,0:T(8,128)(2,1)} fusion(bf16[64,20,128,128]{3,2,1,0:T(8,128)(2,1)} %param.9, bf16[64,20]{1,0:T(8,128)(2,1)S(1)} %fusion.25), kind=kLoop, calls=%fused_computation.25 | loop fusion | flops 20971520 | bytes 83888640 | tf_op jit(solution)/shard_map/mul | solution.py:33
  57.2 163.7 %collective-permute-done = bf16[6,96,64,128]{3,1,2,0:T(8,128)(2,1)} collective-permute-done((bf16[6,96,64,128]{3,1,2,0:T(8,128)(2,1)}, bf16[6,96,64,128]{3,1,2,0:T(8,128)(2,1)}, u32[]{:S(2)}, u32[]{:S(2)}) %collective-permute-start) | collective-permute-done | bytes 9437216 | tf_op jit(solution)/shard_map/ppermute | solution.py:15
  220.9 9.0 constant_dynamic-update-slice_fusion.2
  229.9 13.3 %constant_dynamic-update-slice_fusion.1 = bf16[6,96,192,128]{3,1,2,0:T(8,128)(2,1)} fusion(bf16[6,96,192,128]{3,1,2,0:T(8,128)(2,1)} %constant_dynamic-update-slice_fusion.2, bf16[6,96,64,128]{3,2,1,0:T(8,128)(2,1)} %param.8), kind=kLoop, calls=%fused_computation.49 | loop fusion | bytes 18874368
  243.2 9.0 constant_dynamic-update-slice_fusion
  252.2 24.5 %gather_fusion.2 = bf16[256,6,96,128]{3,2,1,0:T(8,128)(2,1)} fusion(bf16[6,96,192,128]{3,1,2,0:T(8,128)(2,1)} %constant_dynamic-update-slice_fusion, s32[1024]{0:T(1024)S(1)} %get-tuple-element.18), kind=kCustom, calls=%fused_computation.2.clone | custom fusion | bytes 75498496 | tf_op jit(solution)/shard_map/jit(_take)/gather | solution.py:40
  276.7 24.5 %gather_fusion.1 = bf16[256,6,96,128]{3,2,1,0:T(8,128)(2,1)} fusion(bf16[6,96,192,128]{3,1,2,0:T(8,128)(2,1)} %constant_dynamic-update-slice_fusion, s32[1024]{0:T(1024)S(1)} %get-tuple-element.19), kind=kCustom, calls=%fused_computation.1.clone | custom fusion | bytes 75498496 | tf_op jit(solution)/shard_map/jit(_take)/gather | solution.py:40
  301.2 24.3 %gather_fusion.3 = bf16[256,6,96,128]{3,2,1,0:T(8,128)(2,1)} fusion(bf16[6,96,192,128]{3,1,2,0:T(8,128)(2,1)} %constant_dynamic-update-slice_fusion, s32[1024]{0:T(1024)S(1)} %get-tuple-element.17), kind=kCustom, calls=%fused_computation.3.clone | custom fusion | bytes 75498496 | tf_op jit(solution)/shard_map/jit(_take)/gather | solution.py:40
  325.5 24.3 %gather_fusion = bf16[256,6,96,128]{3,2,1,0:T(8,128)(2,1)} fusion(bf16[6,96,192,128]{3,1,2,0:T(8,128)(2,1)} %constant_dynamic-update-slice_fusion, s32[1024]{0:T(1024)S(1)} %pad_clamp_fusion.4), kind=kCustom, calls=%fused_computation.clone | custom fusion | bytes 75498496 | tf_op jit(solution)/shard_map/jit(_take)/gather | solution.py:40
  349.8 24.4 %gather_fusion.4 = bf16[256,6,96,128]{3,2,1,0:T(8,128)(2,1)} fusion(bf16[6,96,192,128]{3,1,2,0:T(8,128)(2,1)} %constant_dynamic-update-slice_fusion, s32[1024]{0:T(1024)S(1)} %get-tuple-element.16), kind=kCustom, calls=%fused_computation.4.clone | custom fusion | bytes 75498496 | tf_op jit(solution)/shard_map/jit(_take)/gather | solution.py:40
  374.2 22.9 %fusion.4 = f32[64,128,6,96,1]{1,3,4,2,0:T(8,128)} fusion(bf16[64,4,6,96,128]{4,3,2,1,0:T(8,128)(2,1)} %bitcast.110, pred[64,4]{1,0:T(8,128)(4,1)S(1)} %copy.77, bf16[64,20,128,128]{3,2,1,0:T(8,128)(2,1)} %broadcast_multiply_fusion), kind=kOutput, calls=%fused_computation.9 | convolution fusion | flops 4850712576 | bytes 65011968 | tf_op jit(solution)/shard_map/ijasd,asdb->ijab/dot_general | solution.py:42
  397.1 22.8 %fusion.6 = f32[64,128,6,96,1]{1,3,4,2,0:T(8,128)} fusion(bf16[64,4,6,96,128]{4,3,2,1,0:T(8,128)(2,1)} %bitcast.111, pred[64,4]{1,0:T(8,128)(4,1)S(1)} %copy-done.1, bf16[64,20,128,128]{3,2,1,0:T(8,128)(2,1)} %broadcast_multiply_fusion), kind=kOutput, calls=%fused_computation.11 | convolution fusion | flops 4850712576 | bytes 65011968 | tf_op jit(solution)/shard_map/ijasd,asdb->ijab/dot_general | solution.py:42
  419.9 23.2 %fusion.2 = f32[64,128,6,96,1]{1,3,4,2,0:T(8,128)} fusion(bf16[64,4,6,96,128]{4,3,2,1,0:T(8,128)(2,1)} %bitcast.109, pred[64,4]{1,0:T(8,128)(4,1)S(1)} %copy-done.2, bf16[64,20,128,128]{3,2,1,0:T(8,128)(2,1)} %broadcast_multiply_fusion), kind=kOutput, calls=%fused_computation.7 | convolution fusion | flops 4850712576 | bytes 65011968 | tf_op jit(solution)/shard_map/ijasd,asdb->ijab/dot_general | solution.py:42
  443.0 22.8 %fusion.8 = f32[64,128,6,96,1]{1,3,4,2,0:T(8,128)} fusion(bf16[64,4,6,96,128]{4,3,2,1,0:T(8,128)(2,1)} %bitcast.108, pred[64,4]{1,0:T(8,128)(4,1)S(1)} %copy-done.3, bf16[64,20,128,128]{3,2,1,0:T(8,128)(2,1)} %broadcast_multiply_fusion), kind=kOutput, calls=%fused_computation.13 | convolution fusion | flops 4850712576 | bytes 65011968 | tf_op jit(solution)/shard_map/ijasd,asdb->ijab/dot_general | solution.py:42
  465.8 45.3 %fusion.17 = f32[6,96,64,128]{3,1,0,2:T(8,128)} fusion(f32[64,128,6,96,1]{1,3,4,2,0:T(8,128)} %fusion.2, f32[64,128,6,96,1]{1,3,4,2,0:T(8,128)} %fusion.4, f32[64,128,6,96,1]{1,3,4,2,0:T(8,128)} %fusion.6, f32[64,128,6,96,1]{1,3,4,2,0:T(8,128)} %fusion.8, bf16[64,4,6,96,128]{4,3,2,1,0:T(8,128)(2,1)} %bitcast.104, pred[64,4]{1,0:T(8,128)(4,1)S(1)} %copy-done, ...), kind=kOutput, calls=%fused_computation.30 | convolution fusion | flops 4869586944 | bytes 140509440 | tf_op jit(solution)/shard_map/ijasd,asdb->ijab/dot_general | solution.py:42
  511.1 12.4 copy.86
  523.5 412.4 %all_to_all.36 = f32[6,96,64,128]{3,2,0,1:T(8,128)S(1)} all-to-all(f32[6,96,64,128]{3,2,0,1:T(8,128)S(1)} %copy.86), channel_id=1, replica_groups=mesh['pair'=16,'virt'=2] {'pair'}, dimensions={1} | all-to-all | bytes 37748736 | tf_op jit(solution)/shard_map/all_to_all | solution.py:45
  935.9 7.4 copy.88
  943.4 22.8 %copy.89 = f32[96,6,64,128]{0,2,1,3:T(8,128)} copy(f32[96,6,64,128]{3,2,1,0:T(8,128)} %bitcast.107) | data formatting | bytes 37748736 | tf_op jit(solution)/shard_map/all_to_all | solution.py:45
  966.2 11.9 all-to-all-start.1
  978.1 0.1 dynamic_slice.7
  978.2 0.1 dynamic_slice.6
  978.3 0.1 broadcast_subtract_fusion
  978.5 273.3 %all-to-all-done.1 = f32[96,6,64,128]{0,2,1,3:T(8,128)} async-done(((f32[96,6,64,128]{0,2,1,3:T(8,128)}), f32[96,6,64,128]{0,2,1,3:T(8,128)}, u32[]{:S(2)}, u32[]{:S(2)}) %all-to-all-start.1) | async-done | bytes 18874400 | tf_op jit(solution)/shard_map/all_to_all | solution.py:44
  1251.8 24.9 %copy.91 = f32[96,6,2,64,64]{0,4,3,2,1:T(8,128)} copy(f32[96,6,2,64,64]{0,3,1,4,2:T(8,128)} %bitcast.37) | data formatting | bytes 37748736 | tf_op jit(solution)/shard_map/all_to_all | solution.py:44
  1276.7 22.6 %copy.92 = f32[96,6,128,64]{2,0,1,3:T(8,128)} copy(f32[96,6,128,64]{0,3,2,1:T(8,128)} %bitcast.105) | data formatting | bytes 37748736 | tf_op jit(solution)/shard_map/all_to_all | solution.py:44
  1299.3 16.9 %fusion.16 = bf16[6,96,64,128]{3,1,0,2:T(8,128)(2,1)} fusion(f32[6,96,64,128]{3,1,0,2:T(8,128)} %fusion.17, f32[96,6,128,64]{2,0,1,3:T(8,128)} %copy.92, f32[128]{0:T(128)S(1)} %copy-done.4, f32[6,96,64]{1,0,2:T(8,128)S(1)} %broadcast_subtract_fusion), kind=kLoop, calls=%fused_computation.28 | loop fusion | flops 18874368 | bytes 47333888 | tf_op jit(solution)/shard_map/convert_element_type | solution.py:60
  1316.2 13.5 %copy.93 = bf16[6,96,64,128]{3,2,1,0:T(8,128)(2,1)} copy(bf16[6,96,64,128]{3,1,0,2:T(8,128)(2,1)} %fusion.16) | data formatting | bytes 18874368 | tf_op jit(solution)/shard_map/convert_element_type | solution.py:60
  (19 shorter events, 0.1 us)
Async XLA Ops:
  13.5 207.4 %collective-permute-start = (bf16[6,96,64,128]{3,1,2,0:T(8,128)(2,1)}, bf16[6,96,64,128]{3,1,2,0:T(8,128)(2,1)}, u32[]{:S(2)}, u32[]{:S(2)}) collective-permute-start(bf16[6,96,64,128]{3,1,2,0:T(8,128)(2,1)} %copy.69), channel_id=1, source_target_pairs={{0,1},{2,3},{4,5},{6,7},{8,9},{10,11},{12,13},{14,15},{16,17},{18,... | collective-permute-start | bytes 28311560 | tf_op jit(solution)/shard_map/ppermute | solution.py:15
  22.0 221.1 %collective-permute-start.1 = (bf16[6,96,64,128]{3,1,2,0:T(8,128)(2,1)}, bf16[6,96,64,128]{3,1,2,0:T(8,128)(2,1)}, u32[]{:S(2)}, u32[]{:S(2)}) collective-permute-start(bf16[6,96,64,128]{3,1,2,0:T(8,128)(2,1)} %copy.69), channel_id=1, source_target_pairs={{1,0},{3,2},{5,4},{7,6},{9,8},{11,10},{13,12},{15,14},{17,16},{19,... | collective-permute-start | bytes 28311560 | tf_op jit(solution)/shard_map/ppermute | solution.py:17
  374.2 22.9 %copy-start.1 = (pred[64,4]{1,0:T(8,128)(4,1)S(1)}, pred[64,4]{1,0:T(8,128)(4,1)}, u32[]{:S(2)}) copy-start(pred[64,4]{1,0:T(8,128)(4,1)} %copy.74) | copy-start | bytes 772
  397.1 22.8 %copy-start.2 = (pred[64,4]{1,0:T(8,128)(4,1)S(1)}, pred[64,4]{1,0:T(8,128)(4,1)}, u32[]{:S(2)}) copy-start(pred[64,4]{1,0:T(8,128)(4,1)} %copy.80) | copy-start | bytes 772
  419.9 23.2 %copy-start.3 = (pred[64,4]{1,0:T(8,128)(4,1)S(1)}, pred[64,4]{1,0:T(8,128)(4,1)}, u32[]{:S(2)}) copy-start(pred[64,4]{1,0:T(8,128)(4,1)} %copy.68) | copy-start | bytes 772
  443.0 22.8 %copy-start = (pred[64,4]{1,0:T(8,128)(4,1)S(1)}, pred[64,4]{1,0:T(8,128)(4,1)}, u32[]{:S(2)}) copy-start(pred[64,4]{1,0:T(8,128)(4,1)} %copy.83) | copy-start | bytes 772
  966.2 11.9 copy-start.4
  966.2 12.0 copy-start.5
  966.2 285.6 %all-to-all-start.1 = ((f32[96,6,64,128]{0,2,1,3:T(8,128)}), f32[96,6,64,128]{0,2,1,3:T(8,128)}, u32[]{:S(2)}, u32[]{:S(2)}) async-start(f32[96,6,64,128]{0,2,1,3:T(8,128)} %copy.89), calls=%async_computation.1 | async-start | bytes 50331648 | tf_op jit(solution)/shard_map/all_to_all | solution.py:44
where the time goes:
time: 1340 us; the launch traced here: 1330 us
  waiting for transfers between devices  437 us (33%)
  blocking collectives  412 us (31%)
  local copies, waits for them, and re-layouts  275 us (21%)
  matrix products  137 us (10%)
  other arithmetic  46.8 us (3%)
  starting transfers between devices  21.9 us (2%)
    all_to_all x1, blocking collectives, per_device(): lax.all_to_all(ladder, 'pair', split_axis=1, concat_axis=0, tiled=True)  412 us
    all_to_all x1, waiting for transfers between devices, per_device(): lax.all_to_all(lax.all_to_all(ladder, 'pair', split_axis=1, concat_axis=0...  273 us
    ppermute x1, waiting for transfers between devices, extended(): lax.ppermute(tail, axis, [(i, (i + 1) % count) for i in range(ends)])  164 us
    dot_general x5, matrix products, per_device(): jnp.einsum('ijasd,asdb->ijab', picked, weights, preferred_element_type=jn...  137 us
    gather x5, local copies, waits for them, and re-layouts, per_device(): picked = jnp.take(padded, columns, axis=2)  122 us
    all_to_all x2, local copies, waits for them, and re-layouts, per_device(): lax.all_to_all(lax.all_to_all(ladder, 'pair', split_axis=1, concat_axis=0...  47.5 us
    unnamed x15, local copies, waits for them, and re-layouts  35.8 us
    all_to_all x2, local copies, waits for them, and re-layouts, per_device(): lax.all_to_all(ladder, 'pair', split_axis=1, concat_axis=0, tiled=True)  30.3 us
  transfers between devices with their start and end apart: 3, of which 2 were waited for; matrix products, arithmetic and copies ran while one was open for 4% of the time, Pallas kernels for 0%

commit v1 on v0

--- a/solution.py
+++ b/solution.py
@@ -2,6 +2,12 @@
 import jax.numpy as jnp
 from jax import lax
 from jax.sharding import PartitionSpec as P
+
+
+def trade_parts(x, mesh_axis, split, join):
+    pieces = jnp.split(x, lax.axis_size(mesh_axis), axis=split)
+    received = lax.all_to_all(jnp.stack(pieces), mesh_axis, 0, 0)
+    return jnp.concatenate(received, axis=join)
 
 
 def extended(cells, sides, width):
@@ -41,12 +47,8 @@
         weights = masked_weights[:, block_start:block_stop]
         term = jnp.einsum("ijasd,asdb->ijab", picked, weights, preferred_element_type=jnp.float32)
         ladder = term if ladder is None else ladder + term
-    arrived_ladder = lax.all_to_all(
-        lax.all_to_all(ladder, "pair", split_axis=1, concat_axis=0, tiled=True),
-        "virt",
-        split_axis=3,
-        concat_axis=2,
-        tiled=True,
+    arrived_ladder = trade_parts(
+        lax.all_to_all(ladder, "pair", split_axis=1, concat_axis=0, tiled=True), "virt", 3, 2
     )
     partner = jnp.transpose(arrived_ladder, (1, 0, 3, 2))
     occupied_own = lax.dynamic_slice_in_dim(eps_occ, first_row, own_rows)

time: 1340 us -> 1380 us (1.030)
  other arithmetic: 46.8 us -> 76.2 us
  local copies, waits for them, and re-layouts: 275 us -> 292 us
    another operation x0 -> x2, local copies, waits for them, and re-layouts: none -> 47.7 us  [trade_parts(): received = lax.all_to_all(jnp.stack(pieces), mesh_axis, 0, 0)]
    all_to_all x2 -> x0, local copies, waits for them, and re-layouts: 47.5 us -> none  [per_device(): lax.all_to_all(lax.all_to_all(ladder, 'pair', split_axis=1, concat_axis=0...]
    reshape x0 -> x2, local copies, waits for them, and re-layouts: none -> 40.2 us  [trade_parts(): return jnp.concatenate(received, axis=join)]
    another operation x0 -> x1, other arithmetic: none -> 29.3 us  [trade_parts(): received = lax.all_to_all(jnp.stack(pieces), mesh_axis, 0, 0)]
    all_to_all x2 -> x1, local copies, waits for them, and re-layouts: 30.3 us -> 7.15 us  [per_device(): lax.all_to_all(ladder, 'pair', split_axis=1, concat_axis=0, tiled=True)]
where the time goes in v1:
time: 1380 us
  waiting for transfers between devices  437 us (32%)
  blocking collectives  413 us (30%)
  local copies, waits for them, and re-layouts  292 us (21%)
  matrix products  137 us (10%)
  other arithmetic  76.2 us (6%)
  starting transfers between devices  21.9 us (2%)
    all_to_all x1, blocking collectives, per_device(): lax.all_to_all(ladder, 'pair', split_axis=1, concat_axis=0, tiled=True)  413 us
    all_to_all x1, waiting for transfers between devices, trade_parts(): received = lax.all_to_all(jnp.stack(pieces), mesh_axis, 0, 0)  273 us
    ppermute x1, waiting for transfers between devices, extended(): lax.ppermute(tail, axis, [(i, (i + 1) % count) for i in range(ends)])  164 us
    dot_general x5, matrix products, per_device(): jnp.einsum('ijasd,asdb->ijab', picked, weights, preferred_element_type=jn...  137 us
    gather x5, local copies, waits for them, and re-layouts, per_device(): picked = jnp.take(padded, columns, axis=2)  122 us
    another operation x2, local copies, waits for them, and re-layouts, trade_parts(): received = lax.all_to_all(jnp.stack(pieces), mesh_axis, 0, 0)  47.7 us
    reshape x2, local copies, waits for them, and re-layouts, trade_parts(): return jnp.concatenate(received, axis=join)  40.2 us
    unnamed x15, local copies, waits for them, and re-layouts  35.8 us
  transfers between devices with their start and end apart: 3, of which 2 were waited for; matrix products, arithmetic and copies ran while one was open for 4% of the time, Pallas kernels for 0%

profile of v1, /device:TPU:0, one launch (start us, length us, event | category | flops | bytes accessed | tf_op | source)
XLA Modules:
  0.0 1376.9 jit_solution(3564846082216690885)
XLA Ops:
  0.0 13.5 copy.69
  13.5 8.6 collective-permute-start
  22.1 1.5 collective-permute-start.1
  23.5 0.7 subtract_add_fusion
  24.3 0.1 copy.75
  24.4 0.1 reshape.127
  24.5 0.1 copy.78
  24.6 0.1 reshape.131
  24.7 0.1 copy.77
  24.8 0.7 copy.74
  25.5 0.1 copy.81
  25.6 0.1 reshape.135
  25.7 0.1 copy.84
  25.8 0.1 reshape.139
  25.9 0.7 copy.80
  26.6 0.1 copy.72
  26.7 0.1 reshape.123
  26.8 0.7 copy.68
  27.5 0.7 copy.83
  28.2 0.7 fusion.25
  29.0 28.2 %broadcast_multiply_fusion = bf16[64,20,128,128]{3,2,1,0:T(8,128)(2,1)} fusion(bf16[64,20,128,128]{3,2,1,0:T(8,128)(2,1)} %param.9, bf16[64,20]{1,0:T(8,128)(2,1)S(1)} %fusion.25), kind=kLoop, calls=%fused_computation.26 | loop fusion | flops 20971520 | bytes 83888640 | tf_op jit(solution)/shard_map/mul | solution.py:39
  57.2 163.7 %collective-permute-done = bf16[6,96,64,128]{3,1,2,0:T(8,128)(2,1)} collective-permute-done((bf16[6,96,64,128]{3,1,2,0:T(8,128)(2,1)}, bf16[6,96,64,128]{3,1,2,0:T(8,128)(2,1)}, u32[]{:S(2)}, u32[]{:S(2)}) %collective-permute-start) | collective-permute-done | bytes 9437216 | tf_op jit(solution)/shard_map/ppermute | solution.py:21
  220.9 9.0 constant_dynamic-update-slice_fusion.2
  229.9 13.3 constant_dynamic-update-slice_fusion.1
  243.2 9.0 constant_dynamic-update-slice_fusion
  252.2 24.5 %gather_fusion.2 = bf16[256,6,96,128]{3,2,1,0:T(8,128)(2,1)} fusion(bf16[6,96,192,128]{3,1,2,0:T(8,128)(2,1)} %constant_dynamic-update-slice_fusion, s32[1024]{0:T(1024)S(1)} %get-tuple-element.20), kind=kCustom, calls=%fused_computation.2.clone | custom fusion | bytes 75498496 | tf_op jit(solution)/shard_map/jit(_take)/gather | solution.py:46
  276.7 24.5 %gather_fusion.1 = bf16[256,6,96,128]{3,2,1,0:T(8,128)(2,1)} fusion(bf16[6,96,192,128]{3,1,2,0:T(8,128)(2,1)} %constant_dynamic-update-slice_fusion, s32[1024]{0:T(1024)S(1)} %get-tuple-element.21), kind=kCustom, calls=%fused_computation.1.clone | custom fusion | bytes 75498496 | tf_op jit(solution)/shard_map/jit(_take)/gather | solution.py:46
  301.2 24.3 %gather_fusion.3 = bf16[256,6,96,128]{3,2,1,0:T(8,128)(2,1)} fusion(bf16[6,96,192,128]{3,1,2,0:T(8,128)(2,1)} %constant_dynamic-update-slice_fusion, s32[1024]{0:T(1024)S(1)} %get-tuple-element.19), kind=kCustom, calls=%fused_computation.3.clone | custom fusion | bytes 75498496 | tf_op jit(solution)/shard_map/jit(_take)/gather | solution.py:46
  325.5 24.3 %gather_fusion = bf16[256,6,96,128]{3,2,1,0:T(8,128)(2,1)} fusion(bf16[6,96,192,128]{3,1,2,0:T(8,128)(2,1)} %constant_dynamic-update-slice_fusion, s32[1024]{0:T(1024)S(1)} %pad_clamp_fusion.4), kind=kCustom, calls=%fused_computation.clone | custom fusion | bytes 75498496 | tf_op jit(solution)/shard_map/jit(_take)/gather | solution.py:46
  349.8 24.4 %gather_fusion.4 = bf16[256,6,96,128]{3,2,1,0:T(8,128)(2,1)} fusion(bf16[6,96,192,128]{3,1,2,0:T(8,128)(2,1)} %constant_dynamic-update-slice_fusion, s32[1024]{0:T(1024)S(1)} %get-tuple-element.18), kind=kCustom, calls=%fused_computation.4.clone | custom fusion | bytes 75498496 | tf_op jit(solution)/shard_map/jit(_take)/gather | solution.py:46
  374.3 22.9 %fusion.4 = f32[64,128,6,96,1]{1,3,4,2,0:T(8,128)} fusion(bf16[64,4,6,96,128]{4,3,2,1,0:T(8,128)(2,1)} %bitcast.112, pred[64,4]{1,0:T(8,128)(4,1)S(1)} %copy.77, bf16[64,20,128,128]{3,2,1,0:T(8,128)(2,1)} %broadcast_multiply_fusion), kind=kOutput, calls=%fused_computation.10 | convolution fusion | flops 4850712576 | bytes 65011968 | tf_op jit(solution)/shard_map/ijasd,asdb->ijab/dot_general | solution.py:48
  397.1 22.8 %fusion.6 = f32[64,128,6,96,1]{1,3,4,2,0:T(8,128)} fusion(bf16[64,4,6,96,128]{4,3,2,1,0:T(8,128)(2,1)} %bitcast.113, pred[64,4]{1,0:T(8,128)(4,1)S(1)} %copy-done.1, bf16[64,20,128,128]{3,2,1,0:T(8,128)(2,1)} %broadcast_multiply_fusion), kind=kOutput, calls=%fused_computation.12 | convolution fusion | flops 4850712576 | bytes 65011968 | tf_op jit(solution)/shard_map/ijasd,asdb->ijab/dot_general | solution.py:48
  419.9 23.1 %fusion.2 = f32[64,128,6,96,1]{1,3,4,2,0:T(8,128)} fusion(bf16[64,4,6,96,128]{4,3,2,1,0:T(8,128)(2,1)} %bitcast.111, pred[64,4]{1,0:T(8,128)(4,1)S(1)} %copy-done.2, bf16[64,20,128,128]{3,2,1,0:T(8,128)(2,1)} %broadcast_multiply_fusion), kind=kOutput, calls=%fused_computation.8 | convolution fusion | flops 4850712576 | bytes 65011968 | tf_op jit(solution)/shard_map/ijasd,asdb->ijab/dot_general | solution.py:48
  443.1 22.8 %fusion.8 = f32[64,128,6,96,1]{1,3,4,2,0:T(8,128)} fusion(bf16[64,4,6,96,128]{4,3,2,1,0:T(8,128)(2,1)} %bitcast.110, pred[64,4]{1,0:T(8,128)(4,1)S(1)} %copy-done.3, bf16[64,20,128,128]{3,2,1,0:T(8,128)(2,1)} %broadcast_multiply_fusion), kind=kOutput, calls=%fused_computation.14 | convolution fusion | flops 4850712576 | bytes 65011968 | tf_op jit(solution)/shard_map/ijasd,asdb->ijab/dot_general | solution.py:48
  465.9 45.4 %fusion.17 = f32[6,96,64,128]{3,1,0,2:T(8,128)} fusion(f32[64,128,6,96,1]{1,3,4,2,0:T(8,128)} %fusion.2, f32[64,128,6,96,1]{1,3,4,2,0:T(8,128)} %fusion.4, f32[64,128,6,96,1]{1,3,4,2,0:T(8,128)} %fusion.6, f32[64,128,6,96,1]{1,3,4,2,0:T(8,128)} %fusion.8, bf16[64,4,6,96,128]{4,3,2,1,0:T(8,128)(2,1)} %bitcast.106, pred[64,4]{1,0:T(8,128)(4,1)S(1)} %copy-done, ...), kind=kOutput, calls=%fused_computation.33 | convolution fusion | flops 4869586944 | bytes 140509440 | tf_op jit(solution)/shard_map/ijasd,asdb->ijab/dot_general | solution.py:48
  511.3 12.4 copy.86
  523.7 412.7 %all_to_all.23 = f32[6,96,64,128]{3,2,0,1:T(8,128)} all-to-all(f32[6,96,64,128]{3,2,0,1:T(8,128)S(1)} %copy.86), channel_id=1, replica_groups=mesh['pair'=16,'virt'=2] {'pair'}, dimensions={1} | all-to-all | bytes 37748736 | tf_op jit(solution)/shard_map/all_to_all | solution.py:51
  936.4 7.1 copy.88
  943.5 13.4 slice_bitcast_fusion.1
  956.9 29.3 %pad_maximum_fusion = f32[2,96,6,64,64]{4,3,2,1,0:T(8,128)} fusion(f32[1,96,6,64,64]{4,3,2,1,0:T(8,128)} %get-tuple-element.7, f32[1,96,6,64,64]{4,3,2,1,0:T(8,128)} %get-tuple-element.6), kind=kLoop, calls=%fused_computation.5 | loop fusion | flops 4718592 | bytes 37748736 | tf_op jit(solution)/shard_map/stack | solution.py:9
  986.2 34.3 %copy.89 = f32[2,96,6,64,64]{1,4,3,2,0:T(8,128)} copy(f32[2,96,6,64,64]{4,3,2,1,0:T(8,128)} %pad_maximum_fusion) | data formatting | bytes 37748736 | tf_op jit(solution)/shard_map/stack | solution.py:9
  1020.6 11.9 all-to-all-start.1
  1032.7 0.1 broadcast_subtract_fusion
  1032.8 273.3 %all-to-all-done.1 = f32[2,96,6,64,64]{1,4,3,2,0:T(8,128)} async-done(((f32[2,96,6,64,64]{1,4,3,2,0:T(8,128)}), f32[2,96,6,64,64]{1,4,3,2,0:T(8,128)}, u32[]{:S(2)}, u32[]{:S(2)}) %all-to-all-start.1) | async-done | bytes 18874400 | tf_op jit(solution)/shard_map/all_to_all | solution.py:9
  1306.1 17.6 %copy.90 = f32[96,6,2,64,64]{0,4,3,2,1:T(8,128)} copy(f32[96,6,2,64,64]{0,4,3,1,2:T(8,128)} %bitcast.37) | data formatting | bytes 37748736 | tf_op jit(solution)/shard_map/reshape | solution.py:10
  1323.7 22.6 %copy.91 = f32[96,6,128,64]{2,0,1,3:T(8,128)} copy(f32[96,6,128,64]{0,3,2,1:T(8,128)} %bitcast.108) | data formatting | bytes 37748736 | tf_op jit(solution)/shard_map/reshape | solution.py:10
  1346.3 16.9 %fusion.16 = bf16[6,96,64,128]{3,1,0,2:T(8,128)(2,1)} fusion(f32[6,96,64,128]{3,1,0,2:T(8,128)} %fusion.17, f32[96,6,128,64]{2,0,1,3:T(8,128)} %copy.91, f32[128]{0:T(128)S(1)} %copy-done.4, f32[6,96,64]{1,0,2:T(8,128)S(1)} %broadcast_subtract_fusion), kind=kLoop, calls=%fused_computation.31 | loop fusion | flops 18874368 | bytes 47333888 | tf_op jit(solution)/shard_map/convert_element_type | solution.py:62
  1363.2 13.5 copy.92
  (21 shorter events, 0.3 us)
Async XLA Ops:
  13.5 207.4 %collective-permute-start = (bf16[6,96,64,128]{3,1,2,0:T(8,128)(2,1)}, bf16[6,96,64,128]{3,1,2,0:T(8,128)(2,1)}, u32[]{:S(2)}, u32[]{:S(2)}) collective-permute-start(bf16[6,96,64,128]{3,1,2,0:T(8,128)(2,1)} %copy.69), channel_id=1, source_target_pairs={{0,1},{2,3},{4,5},{6,7},{8,9},{10,11},{12,13},{14,15},{16,17},{18,... | collective-permute-start | bytes 28311560 | tf_op jit(solution)/shard_map/ppermute | solution.py:21
  22.1 221.1 %collective-permute-start.1 = (bf16[6,96,64,128]{3,1,2,0:T(8,128)(2,1)}, bf16[6,96,64,128]{3,1,2,0:T(8,128)(2,1)}, u32[]{:S(2)}, u32[]{:S(2)}) collective-permute-start(bf16[6,96,64,128]{3,1,2,0:T(8,128)(2,1)} %copy.69), channel_id=1, source_target_pairs={{1,0},{3,2},{5,4},{7,6},{9,8},{11,10},{13,12},{15,14},{17,16},{19,... | collective-permute-start | bytes 28311560 | tf_op jit(solution)/shard_map/ppermute | solution.py:23
  374.3 22.9 %copy-start.1 = (pred[64,4]{1,0:T(8,128)(4,1)S(1)}, pred[64,4]{1,0:T(8,128)(4,1)}, u32[]{:S(2)}) copy-start(pred[64,4]{1,0:T(8,128)(4,1)} %copy.74) | copy-start | bytes 772
  397.1 22.8 %copy-start.2 = (pred[64,4]{1,0:T(8,128)(4,1)S(1)}, pred[64,4]{1,0:T(8,128)(4,1)}, u32[]{:S(2)}) copy-start(pred[64,4]{1,0:T(8,128)(4,1)} %copy.80) | copy-start | bytes 772
  419.9 23.2 %copy-start.3 = (pred[64,4]{1,0:T(8,128)(4,1)S(1)}, pred[64,4]{1,0:T(8,128)(4,1)}, u32[]{:S(2)}) copy-start(pred[64,4]{1,0:T(8,128)(4,1)} %copy.68) | copy-start | bytes 772
  443.1 22.8 %copy-start = (pred[64,4]{1,0:T(8,128)(4,1)S(1)}, pred[64,4]{1,0:T(8,128)(4,1)}, u32[]{:S(2)}) copy-start(pred[64,4]{1,0:T(8,128)(4,1)} %copy.83) | copy-start | bytes 772
  1020.6 11.9 copy-start.4
  1020.6 12.0 copy-start.5
  1020.6 285.6 %all-to-all-start.1 = ((f32[2,96,6,64,64]{1,4,3,2,0:T(8,128)}), f32[2,96,6,64,64]{1,4,3,2,0:T(8,128)}, u32[]{:S(2)}, u32[]{:S(2)}) async-start(f32[2,96,6,64,64]{1,4,3,2,0:T(8,128)} %copy.89), calls=%async_computation.1 | async-start | bytes 50331648 | tf_op jit(solution)/shard_map/all_to_all | solution.py:9
